TPU v7x, 256 devices: a whole 4x4x8 slice. The times are simulated.
256 devices in a mesh: seq: 32 (over z, x), mp: 8 (over y, core).
Axes of the slice: x: 4, y: 4, z: 8, core: 2. Of those that a mesh axis runs over, the one named last changes fastest.
Arguments:
- win_query: bfloat16 [16384, 4096], P('seq', 'mp'), may hold values from -8 to 8
- win_key: bfloat16 [16384, 4096], P('seq', 'mp'), may hold values from -8 to 8
- win_value: bfloat16 [16384, 4096], P('seq', 'mp'), may hold values from -6 to 6
- win_dout: bfloat16 [16384, 4096], P('seq', 'mp'), may hold values from -16 to 16
- cross_query: bfloat16 [16384, 4096], P('seq', 'mp'), may hold values from -8 to 8
- cross_dout: bfloat16 [16384, 4096], P('seq', 'mp'), may hold values from -16 to 16
- patch_key: bfloat16 [4096, 4096], P('seq', 'mp'), may hold values from -8 to 8
- patch_value: bfloat16 [4096, 4096], P('seq', 'mp'), may hold values from -6 to 6
- patch_len: int32 [64, 64], P('seq'), may hold values from 1 to 16, 256 in all within a row
- patch_owner: int32 [4096, 1], P('seq'), may hold values from 0 to 31; in each aligned block of 128 rows (0 to 127, 128 to 255, ...) at most 8 rows name the same one
- w_query: bfloat16 [4096, 4096], P('seq', 'mp'), may hold values from -0.09375 to 0.09375
Outputs:
- win_dq: bfloat16 [16384, 4096], P('seq', 'mp')
- win_dk: bfloat16 [16384, 4096], P('seq', 'mp')
- win_dv: bfloat16 [16384, 4096], P('seq', 'mp')
- patch_grads: bfloat16 [2, 8192, 4096], P(None, 'seq', 'mp')
- byte_grads: bfloat16 [16384, 4096], P('seq', 'mp')
Inputs may be any that keep to these rules, and one draw needn't show every extreme that they name: `patch_len`: each row lists the byte lengths of the patches of one stored block in order; they sum to 256 and the largest is exactly 16. `patch_owner`: within each aligned block of 128 rows (the patch rows of one device) no owner is named more than 8 times, a bound that some block reaches.
All inputs are finite; a program needn't handle non-finite values.
Results may differ from a plain program's by a relative error of at most 0.017.
Values may be sent and summed in bfloat16 or wider, within the bound.
No kernel may reach another device: no remote copies, remote signals or barrier semaphores. Data moves between devices by JAX's collectives and lax.ppermute only.
A program may use at most 64 MiB of HBM per device.

v0:
```python
import math
import jax
import jax.numpy as jnp
from jax import lax
from jax.sharding import PartitionSpec as P

HD = 128
WIN = 256


def shifted(block, axis, distance):
    devices = range(lax.axis_size(axis))
    route = [(i - distance, i) for i in devices if i - distance in devices]
    return lax.ppermute(block, axis, route)


def head_split(values):
    return values.reshape(values.shape[0], values.shape[1] // HD, HD)


def row_stats(scores, allowed):
    masked = jnp.where(allowed, scores, -1e30)
    row_top = jnp.max(masked, axis=-1, keepdims=True)
    row_total = jnp.sum(
        jnp.exp(jnp.where(allowed, scores - row_top, -1e30)), axis=-1, keepdims=True
    )
    return row_top + jnp.log(row_total)


def window_part(query_rows, dout_rows, key_ext, value_ext, tail_valid):
    window = WIN
    inv_root = 1.0 / math.sqrt(HD)
    length = query_rows.shape[0]
    width = query_rows.shape[1]
    head_count = width // HD
    query_heads = head_split(query_rows)
    dout_heads = head_split(dout_rows)
    key_heads = head_split(key_ext)
    value_heads = head_split(value_ext)
    rows_at = lax.broadcasted_iota(jnp.int32, (window, 2 * window), 0)
    cols_at = lax.broadcasted_iota(jnp.int32, (window, 2 * window), 1)
    gap = cols_at - rows_at

    def one_step(sub_step, state_in):
        dq_acc, dk_acc, dv_acc, total_acc, delta_acc = state_in
        offset = sub_step * window
        allowed = ((gap >= 0) & (gap <= window) & ((cols_at + offset >= window) | tail_valid))[None]
        scores = (
            jnp.einsum("qhd,khd->hqk", query_heads, key_heads, preferred_element_type=jnp.float32)
            * inv_root
        )
        log_total = row_stats(scores, allowed)
        prob_rows = jnp.exp(jnp.where(allowed, scores - log_total, -1e30))
        dprobs = jnp.einsum(
            "qhd,khd->hqk", dout_heads, value_heads, preferred_element_type=jnp.float32
        )
        row_delta = jnp.sum(prob_rows * dprobs, axis=-1, keepdims=True)
        grad_scores = (prob_rows * (dprobs - row_delta) * inv_root).astype(jnp.bfloat16)
        probs_low = prob_rows.astype(jnp.bfloat16)
        dq_sub = jnp.einsum(
            "hqk,khd->qhd", grad_scores, key_heads, preferred_element_type=jnp.float32
        )
        dk_sub = jnp.einsum(
            "hqk,qhd->khd", grad_scores, query_heads, preferred_element_type=jnp.float32
        )
        dv_sub = jnp.einsum(
            "hqk,qhd->khd", probs_low, dout_heads, preferred_element_type=jnp.float32
        )
        dq_acc = dq_sub
        dk_acc = dk_acc + dk_sub
        dv_acc = dv_acc + dv_sub
        total_acc = log_total[:, :, 0].T
        delta_acc = row_delta[:, :, 0].T
        return (dq_acc, dk_acc, dv_acc, total_acc, delta_acc)

    start_state = (
        jnp.zeros((length, head_count, HD), jnp.float32),
        jnp.zeros((length + window, head_count, HD), jnp.float32),
        jnp.zeros((length + window, head_count, HD), jnp.float32),
        jnp.zeros((length, head_count), jnp.float32),
        jnp.zeros((length, head_count), jnp.float32),
    )
    dq_acc, dk_acc, dv_acc, total_acc, delta_acc = lax.fori_loop(
        0, length // window, one_step, start_state
    )
    return (
        dq_acc.reshape(length, width),
        dk_acc.reshape(length + window, width),
        dv_acc.reshape(length + window, width),
        total_acc,
        delta_acc,
    )


def local(
    win_query,
    win_key,
    win_value,
    win_dout,
    cross_query,
    cross_dout,
    patch_key,
    patch_value,
    patch_len,
    patch_owner,
    w_query,
):
    window = WIN
    row_count = win_query.shape[0]
    block_rows = row_count // 2
    width = win_query.shape[1]
    head_count = width // HD
    inv_root = 1.0 / math.sqrt(HD)
    seq_count = lax.axis_size("seq")
    seq_index = lax.axis_index("seq")
    is_last = seq_index == seq_count - 1
    low_valid = seq_index > 0
    low_rim = jnp.stack(
        [win_key[block_rows - window : block_rows], win_value[block_rows - window : block_rows]]
    )
    high_rim = jnp.stack([win_key[row_count - window :], win_value[row_count - window :]])
    from_before = shifted(low_rim, "seq", 1)
    from_after = shifted(high_rim, "seq", -1)
    high_prev = jnp.where(is_last, low_rim, from_after)
    low_part = window_part(
        win_query[:block_rows],
        win_dout[:block_rows],
        jnp.concatenate([from_before[0], win_key[:block_rows]], axis=0),
        jnp.concatenate([from_before[1], win_value[:block_rows]], axis=0),
        low_valid,
    )
    high_part = window_part(
        win_query[block_rows:],
        win_dout[block_rows:],
        jnp.concatenate([high_prev[0], win_key[block_rows:]], axis=0),
        jnp.concatenate([high_prev[1], win_value[block_rows:]], axis=0),
        jnp.array(True),
    )
    low_send = jnp.stack([low_part[1][:window], low_part[2][:window]])
    high_send = jnp.stack([high_part[1][:window], high_part[2][:window]])
    low_back = shifted(low_send.astype(jnp.bfloat16), "seq", -1).astype(low_send.dtype)
    high_back = shifted(high_send.astype(jnp.bfloat16), "seq", 1).astype(high_send.dtype)
    low_extra = low_back + jnp.where(is_last, high_send, 0.0)
    dk_low = low_part[1][window:].at[block_rows - window :].add(low_extra[0])
    dv_low = low_part[2][window:].at[block_rows - window :].add(low_extra[1])
    dk_high = high_part[1][window:].at[block_rows - window :].add(high_back[0])
    dv_high = high_part[2][window:].at[block_rows - window :].add(high_back[1])
    win_dq = jnp.concatenate([low_part[0], high_part[0]], axis=0).astype(jnp.bfloat16)
    win_dk = jnp.concatenate([dk_low, dk_high], axis=0).astype(jnp.bfloat16)
    win_dv = jnp.concatenate([dv_low, dv_high], axis=0).astype(jnp.bfloat16)
    patch_rows = patch_key.shape[0]
    per_block = patch_rows // 2
    cross_heads = cross_query.reshape(2, block_rows, head_count, HD)
    grad_heads = cross_dout.reshape(2, block_rows, head_count, HD)
    key_heads = patch_key.reshape(2, per_block, head_count, HD)
    value_heads = patch_value.reshape(2, per_block, head_count, HD)
    starts = jnp.cumsum(patch_len, axis=1) - patch_len
    within = lax.broadcasted_iota(jnp.int32, (block_rows, per_block), 0)
    allowed = (starts[:, None, :] <= within[None])[:, None]
    scores = (
        jnp.einsum("bqhd,bkhd->bhqk", cross_heads, key_heads, preferred_element_type=jnp.float32)
        * inv_root
    )
    log_total = row_stats(scores, allowed)
    prob_rows = jnp.exp(jnp.where(allowed, scores - log_total, -1e30))
    dprobs = jnp.einsum(
        "bqhd,bkhd->bhqk", grad_heads, value_heads, preferred_element_type=jnp.float32
    )
    row_delta = jnp.sum(prob_rows * dprobs, axis=-1, keepdims=True)
    cross_grad = (prob_rows * (dprobs - row_delta) * inv_root).astype(jnp.bfloat16)
    cross_low = prob_rows.astype(jnp.bfloat16)
    cross_dq = (
        jnp.einsum("bhqk,bkhd->bqhd", cross_grad, key_heads, preferred_element_type=jnp.float32)
        .astype(jnp.bfloat16)
        .reshape(row_count, width)
    )
    patch_dk = (
        jnp.einsum("bhqk,bqhd->bkhd", cross_grad, cross_heads, preferred_element_type=jnp.float32)
        .astype(jnp.bfloat16)
        .reshape(patch_rows, width)
    )
    patch_dv = (
        jnp.einsum("bhqk,bqhd->bkhd", cross_low, grad_heads, preferred_element_type=jnp.float32)
        .astype(jnp.bfloat16)
        .reshape(patch_rows, width)
    )
    stacked = jnp.stack([patch_dk, patch_dv])
    slot_cap = max(2, 2 * (patch_rows // seq_count))
    owners = patch_owner[:, 0]
    onehot = (
        owners[:, None] == lax.broadcasted_iota(jnp.int32, (patch_rows, seq_count), 1)
    ).astype(jnp.int32)
    slot_rank = jnp.sum(onehot * (jnp.cumsum(onehot, axis=0) - onehot), axis=1)
    slot_index = owners * slot_cap + slot_rank
    selector = (
        lax.broadcasted_iota(jnp.int32, (seq_count * slot_cap, patch_rows), 0)
        == slot_index[None, :]
    ).astype(jnp.bfloat16)
    buffer = jnp.einsum(
        "sr,krw->ksw", selector, stacked, preferred_element_type=jnp.float32
    ).astype(jnp.bfloat16)
    buffer = buffer.reshape(2, seq_count, slot_cap, width)
    arrived = lax.all_to_all(buffer, "seq", split_axis=1, concat_axis=1, tiled=True)
    patch_grads = arrived.reshape(2, seq_count * slot_cap, width)
    partial_sums = lax.dot_general(
        cross_dq,
        lax.all_gather(w_query, "seq", axis=0, tiled=True),
        (((1,), (1,)), ((), ())),
        preferred_element_type=jnp.float32,
    )
    byte_grads = lax.psum_scatter(
        partial_sums.astype(jnp.bfloat16), "mp", scatter_dimension=1, tiled=True
    )
    return (win_dq, win_dk, win_dv, patch_grads, byte_grads)


def solution(mesh):
    in_specs = (
        P("seq", "mp"),
        P("seq", "mp"),
        P("seq", "mp"),
        P("seq", "mp"),
        P("seq", "mp"),
        P("seq", "mp"),
        P("seq", "mp"),
        P("seq", "mp"),
        P("seq", None),
        P("seq", None),
        P("seq", "mp"),
    )
    out_specs = (
        P("seq", "mp"),
        P("seq", "mp"),
        P("seq", "mp"),
        P(None, "seq", "mp"),
        P("seq", "mp"),
    )
    return jax.shard_map(local, mesh=mesh, in_specs=in_specs, out_specs=out_specs, check_vma=False)
```

profile of v0, /device:TPU:102, one launch (start us, length us, event | category | flops | bytes accessed | tf_op | source)
XLA Modules:
  0.0 195.4 jit_solution(15188983516557459057)
XLA Ops:
  8.0 1.1 fusion.173
  9.2 1.1 fusion.172
  11.4 2.7 %collective-permute-start.1 = (bf16[2,256,512]{1,2,0:T(8,128)(2,1)}, bf16[2,256,512]{1,2,0:T(8,128)(2,1)S(1)}, u32[]{:S(2)}, u32[]{:S(2)}) collective-permute-start(bf16[2,256,512]{1,2,0:T(8,128)(2,1)} %pad_maximum_fusion.3), channel_id=1, source_target_pairs={{8,0},{16,8},{24,16},{32,24},{40,32},{48,40},{56,48},{64,56},{72,6... | collective-permute-start | bytes 1572872 | tf_op jit(solution)/shard_map/ppermute | solution.py:14
  15.5 1.2 select_reduce_fusion
  16.8 1.1 fusion.106
  17.9 2.5 %fusion.22 = bf16[2,256,4,128]{3,1,2,0:T(8,128)(2,1)} fusion(f32[2,4,256,64]{2,3,1,0:T(8,128)} %fusion.106, f32[2,4,256,64]{2,3,1,0:T(8,128)S(1)} %get-tuple-element.210, f32[2,4,256]{2,1,0:T(4,128)S(1)} %bitcast.241, pred[2,256,64]{1,2,0:T(8,128)(4,1)S(1)} %iota_compare_fusion.1, bf16[2,64,4,128]{3,2,1,0:T(4,128)(2,1)S(1)} %copy-done.12), kind=kOutput, calls=%fused_computation.39 | convolution fusion | flops 34998336 | bytes 1744896 | tf_op jit(solution)/shard_map/bhqk,bkhd->bqhd/dot_general | solution.py:173
  20.4 2.2 %copy.171 = bf16[2,256,4,128]{3,2,1,0:T(4,128)(2,1)} copy(bf16[2,256,4,128]{3,1,2,0:T(8,128)(2,1)} %fusion.22) | data formatting | bytes 1048576 | tf_op jit(solution)/shard_map/convert_element_type | solution.py:174
  22.7 69.5 %all-gather.2.cloned.1.call-done = bf16[4096,512]{1,0:T(8,128)(2,1)} async-done(((bf16[128,512]{1,0:T(8,128)(2,1)}), bf16[4096,512]{1,0:T(8,128)(2,1)}) %all-gather.2.cloned.1.call-update) | async-done | bytes 4194320 | tf_op jit(solution)/shard_map/all_gather | solution.py:207
  92.2 6.7 %convolution_convert_fusion = bf16[512,4096]{1,0:T(8,128)(2,1)} fusion(bf16[4096,512]{1,0:T(8,128)(2,1)} %all-gather.2.cloned.1.call-done, bf16[64,8,4,128]{3,2,1,0:T(4,128)(2,1)} %bitcast.232), kind=kOutput, calls=%fused_computation.3 | convolution fusion | flops 2149580800 | bytes 8912896 | tf_op jit(solution)/shard_map/dot_general | solution.py:205
  99.3 1.6 fusion.27
  101.9 0.9 copy.168
  102.8 8.0 %all-to-all-start = ((bf16[2,32,8,512]{3,2,0,1:T(8,128)(2,1)}), bf16[2,32,8,512]{3,2,0,1:T(8,128)(2,1)S(1)}, u32[]{:S(2)}, u32[]{:S(2)}) async-start(bf16[2,32,8,512]{3,2,0,1:T(8,128)(2,1)} %copy.168), calls=%async_computation | async-start | bytes 1048576 | tf_op jit(solution)/shard_map/all_to_all | solution.py:203
  110.8 1.1 fusion.170
  111.9 1.1 fusion.169
  113.1 0.8 copy.149
  114.2 0.8 copy.192
  116.0 0.9 copy.137
  116.9 0.8 copy.188
  119.4 0.9 pad_maximum_fusion.1
  120.3 0.8 copy.148
  121.2 0.8 copy.144
  122.0 1.7 fusion.6
  124.2 1.8 fusion.98
  125.9 1.7 convolution_bitcast_fusion
  127.7 3.8 %convolution_convert_fusion.3 = bf16[4,256,128]{1,2,0:T(8,128)(2,1)S(1)} fusion(f32[4,512,256]{2,1,0:T(8,128)} %fusion.98, f32[4,512,256]{2,1,0:T(8,128)S(1)} %get-tuple-element.206, f32[4,256]{1,0:T(4,128)S(1)} %log_add_fusion.1, pred[256,512]{0,1:T(8,128)(4,1)S(1)} %copy-done.3, bf16[256,4,128]{2,0,1:T(8,128)(2,1)} %copy.145, bf16[256,4,128]{2,0,1:T(8,128)(2,1)} %copy.144), kind=kOutput, calls=%fused_computation.45 | convolution fusion | flops 141166080 | bytes 5115904 | tf_op jit(solution)/shard_map/while/body/eval_jaxpr/hqk,khd->qhd/dot_general | solution.py:60
  131.5 0.8 copy.155
  132.4 4.7 %collective-permute-start = (bf16[2,256,512]{1,2,0:T(8,128)(2,1)}, bf16[2,256,512]{1,2,0:T(8,128)(2,1)}, u32[]{:S(2)}, u32[]{:S(2)}) collective-permute-start(bf16[2,256,512]{1,2,0:T(8,128)(2,1)} %get-tuple-element.195), channel_id=1, source_target_pairs={{0,8},{8,16},{16,24},{24,32},{32,40},{40,48},{48,56},{56,64},{64,7... | collective-permute-start | bytes 1572872 | tf_op jit(solution)/shard_map/ppermute | solution.py:14
  137.1 2.1 %fusion.166 = (f32[256,4,128]{0,2,1:T(8,128)}, f32[256,4,128]{0,2,1:T(8,128)S(1)}) fusion(f32[512,4,128]{0,2,1:T(8,128)} %convolution_bitcast_fusion), kind=kLoop, calls=%fused_computation.190 | loop fusion | bytes 2097152 | tf_op jit(solution)/shard_map/slice | solution.py:147
  139.2 5.0 %convolution_bitcast_fusion.1 = f32[512,4,128]{0,2,1:T(8,128)} fusion(bf16[256,4,128]{0,2,1:T(8,128)(2,1)} %bitcast.236, f32[4,512,256]{2,1,0:T(8,128)} %fusion.98, f32[4,512,256]{2,1,0:T(8,128)S(1)} %get-tuple-element.206, f32[4,256]{1,0:T(4,128)S(1)} %log_add_fusion.1, pred[256,512]{0,1:T(8,128)(4,1)} %fusion.104), kind=kOutput, calls=%fused_computation.33 | convolution fusion | flops 139986432 | bytes 5640192 | tf_op jit(solution)/shard_map/while/body/eval_jaxpr/hqk,qhd->khd/dot_general | solution.py:63
  144.2 2.1 %fusion.167 = (f32[256,4,128]{0,2,1:T(8,128)}, f32[256,4,128]{0,2,1:T(8,128)S(1)}) fusion(f32[512,4,128]{0,2,1:T(8,128)} %convolution_bitcast_fusion.1), kind=kLoop, calls=%fused_computation.191 | loop fusion | bytes 2097152 | tf_op jit(solution)/shard_map/slice | solution.py:146
  146.3 0.9 fusion.83
  147.2 3.3 %collective-permute-start.3 = (bf16[2,256,512]{1,2,0:T(8,128)(2,1)}, bf16[2,256,512]{1,2,0:T(8,128)(2,1)}, u32[]{:S(2)}, u32[]{:S(2)}) collective-permute-start(bf16[2,256,512]{1,2,0:T(8,128)(2,1)} %fusion.83), channel_id=1, source_target_pairs={{0,8},{8,16},{16,24},{24,32},{32,40},{40,48},{48,56},{56,64},{64,7... | collective-permute-start | bytes 1572872 | tf_op jit(solution)/shard_map/ppermute | solution.py:14
  151.4 1.8 fusion.168
  154.0 1.6 fusion.15
  157.5 0.8 slice.190
  158.3 1.8 copy.136
  160.1 2.8 %fusion.94 = f32[4,512,256]{2,1,0:T(8,128)} fusion(bf16[256,4,128]{0,2,1:T(8,128)(2,1)S(1)} %bitcast.222, bf16[256,4,128]{2,0,1:T(8,128)(2,1)} %copy.137, bf16[256,4,128]{2,0,1:T(8,128)(2,1)} %copy.136), kind=kOutput, calls=%fused_computation.107 | convolution fusion | flops 135266304 | bytes 2883584 | tf_op jit(solution)/shard_map/while/body/eval_jaxpr/qhd,khd->hqk/dot_general | solution.py:54
  163.0 4.7 %convolution_bitcast_fusion.3 = f32[512,4,128]{0,2,1:T(8,128)} fusion(bf16[256,4,128]{0,2,1:T(8,128)(2,1)} %bitcast.234, f32[4,512,256]{2,1,0:T(8,128)} %fusion.94, f32[4,512,256]{2,1,0:T(8,128)S(1)} %get-tuple-element.208, f32[4,256]{1,0:T(4,128)S(1)} %log_add_fusion.2, pred[256,512]{0,1:T(8,128)(4,1)S(1)} %broadcast_and_fusion), kind=kOutput, calls=%fused_computation.35 | convolution fusion | flops 139986432 | bytes 5640192 | tf_op jit(solution)/shard_map/while/body/eval_jaxpr/hqk,qhd->khd/dot_general | solution.py:63
  167.7 1.1 slice.217
  168.8 0.8 pad_maximum_fusion.6
  169.6 2.5 %collective-permute-start.2 = (bf16[2,256,512]{1,2,0:T(8,128)(2,1)}, bf16[2,256,512]{1,2,0:T(8,128)(2,1)}, u32[]{:S(2)}, u32[]{:S(2)}) collective-permute-start(bf16[2,256,512]{1,2,0:T(8,128)(2,1)} %pad_maximum_fusion.6), channel_id=1, source_target_pairs={{8,0},{16,8},{24,16},{32,24},{40,32},{48,40},{56,48},{64,56},{72,6... | collective-permute-start | bytes 1572872 | tf_op jit(solution)/shard_map/ppermute | solution.py:14
  172.1 4.6 %convolution_convert_fusion.4 = bf16[4,128,256]{2,1,0:T(8,128)(2,1)} fusion(f32[4,512,256]{2,1,0:T(8,128)} %fusion.94, f32[4,512,256]{2,1,0:T(8,128)S(1)} %get-tuple-element.208, f32[4,256]{1,0:T(4,128)S(1)} %log_add_fusion.2, pred[256,512]{0,1:T(8,128)(4,1)S(1)} %broadcast_and_fusion, bf16[256,4,128]{2,0,1:T(8,128)(2,1)} %copy.133, ...), kind=kOutput, calls=%fused_computation.46 | convolution fusion | flops 141166080 | bytes 5115904 | tf_op jit(solution)/shard_map/while/body/eval_jaxpr/hqk,khd->qhd/dot_general | solution.py:60
  176.7 1.2 copy.154
  177.9 1.1 convert_element_type.74
  180.1 5.1 %collective-permute-done.2 = bf16[2,256,512]{1,2,0:T(8,128)(2,1)} collective-permute-done((bf16[2,256,512]{1,2,0:T(8,128)(2,1)}, bf16[2,256,512]{1,2,0:T(8,128)(2,1)}, u32[]{:S(2)}, u32[]{:S(2)}) %collective-permute-start.2) | collective-permute-done | bytes 524320 | tf_op jit(solution)/shard_map/ppermute | solution.py:14
  185.1 1.1 select_add_fusion
  186.6 1.0 copy.172
  187.6 1.0 copy.173
  (85 shorter events, 13.1 us)
Async XLA Ops:
  7.2 85.0 %all-gather.2.cloned.1.call-start = ((), (), s32[]{:S(2)}) async-start(), calls=%async_computation.2 | async-start | bytes 4325376 | tf_op jit(solution)/shard_map/all_gather | solution.py:207
  7.9 6.2 %copy-start.8 = (bf16[512,512]{1,0:T(8,128)(2,1)S(1)}, bf16[512,512]{1,0:T(8,128)(2,1)}, u32[]{:S(2)}) copy-start(bf16[512,512]{1,0:T(8,128)(2,1)} %param.32) | copy-start | bytes 1572868
  7.9 180.7 %reduce-scatter.2.cloned.1.call-start = ((), (), s32[]{:S(2)}) async-start(), calls=%async_computation.3 | async-start | bytes 4718592 | tf_op jit(solution)/shard_map/reduce_scatter | solution.py:211
  9.1 5.2 %copy-start.13 = (s32[2,64]{1,0:T(2,128)S(1)}, s32[2,64]{1,0:T(2,128)}, u32[]{:S(2)}) copy-start(s32[2,64]{1,0:T(2,128)} %param.35) | copy-start | bytes 1540
  9.1 5.4 %copy-start.10 = (bf16[128,512]{1,0:T(8,128)(2,1)S(1)}, bf16[128,512]{1,0:T(8,128)(2,1)}, u32[]{:S(2)}) copy-start(bf16[128,512]{1,0:T(8,128)(2,1)} %param.33) | copy-start | bytes 393220
  9.2 6.0 %copy-start.9 = (bf16[512,512]{1,0:T(8,128)(2,1)S(1)}, bf16[512,512]{1,0:T(8,128)(2,1)}, u32[]{:S(2)}) copy-start(bf16[512,512]{1,0:T(8,128)(2,1)} %param.31) | copy-start | bytes 1572868
  10.4 5.0 %copy-start.11 = (bf16[128,512]{1,0:T(8,128)(2,1)S(1)}, bf16[128,512]{1,0:T(8,128)(2,1)}, u32[]{:S(2)}) copy-start(bf16[128,512]{1,0:T(8,128)(2,1)} %param.34) | copy-start | bytes 393220
  11.4 108.0 %collective-permute-start.1 = (bf16[2,256,512]{1,2,0:T(8,128)(2,1)}, bf16[2,256,512]{1,2,0:T(8,128)(2,1)S(1)}, u32[]{:S(2)}, u32[]{:S(2)}) collective-permute-start(bf16[2,256,512]{1,2,0:T(8,128)(2,1)} %pad_maximum_fusion.3), channel_id=1, source_target_pairs={{8,0},{16,8},{24,16},{32,24},{40,32},{48,40},{56,48},{64,56},{72,6... | collective-permute-start | bytes 1572872 | tf_op jit(solution)/shard_map/ppermute | solution.py:14
  15.4 2.6 %copy-start.12 = (bf16[2,64,4,128]{3,2,1,0:T(4,128)(2,1)S(1)}, bf16[2,64,4,128]{3,2,1,0:T(4,128)(2,1)}, u32[]{:S(2)}) copy-start(bf16[2,64,4,128]{3,2,1,0:T(4,128)(2,1)} %reshape.280) | copy-start | bytes 393220
  98.9 2.3 %copy-start.14 = (s32[128,1]{0,1:T(1,128)S(1)}, s32[128,1]{0,1:T(1,128)}, u32[]{:S(2)}) copy-start(s32[128,1]{0,1:T(1,128)} %param.36) | copy-start | bytes 1540
  102.8 47.8 %all-to-all-start = ((bf16[2,32,8,512]{3,2,0,1:T(8,128)(2,1)}), bf16[2,32,8,512]{3,2,0,1:T(8,128)(2,1)S(1)}, u32[]{:S(2)}, u32[]{:S(2)}) async-start(bf16[2,32,8,512]{3,2,0,1:T(8,128)(2,1)} %copy.168), calls=%async_computation | async-start | bytes 1048576 | tf_op jit(solution)/shard_map/all_to_all | solution.py:203
  120.3 1.7 copy-start.3
  122.0 2.1 %copy-start.6 = (bf16[256,4,128]{2,0,1:T(8,128)(2,1)S(1)}, bf16[256,4,128]{2,0,1:T(8,128)(2,1)}, u32[]{:S(2)}) copy-start(bf16[256,4,128]{2,0,1:T(8,128)(2,1)} %copy.149) | copy-start | bytes 786436
  122.0 2.2 %copy-start.7 = (bf16[256,4,128]{2,0,1:T(8,128)(2,1)S(1)}, bf16[256,4,128]{2,0,1:T(8,128)(2,1)}, u32[]{:S(2)}) copy-start(bf16[256,4,128]{2,0,1:T(8,128)(2,1)} %copy.148) | copy-start | bytes 786436
  132.4 19.0 %collective-permute-start = (bf16[2,256,512]{1,2,0:T(8,128)(2,1)}, bf16[2,256,512]{1,2,0:T(8,128)(2,1)}, u32[]{:S(2)}, u32[]{:S(2)}) collective-permute-start(bf16[2,256,512]{1,2,0:T(8,128)(2,1)} %get-tuple-element.195), channel_id=1, source_target_pairs={{0,8},{8,16},{16,24},{24,32},{32,40},{40,48},{48,56},{56,64},{64,7... | collective-permute-start | bytes 1572872 | tf_op jit(solution)/shard_map/ppermute | solution.py:14
  147.2 30.8 %collective-permute-start.3 = (bf16[2,256,512]{1,2,0:T(8,128)(2,1)}, bf16[2,256,512]{1,2,0:T(8,128)(2,1)}, u32[]{:S(2)}, u32[]{:S(2)}) collective-permute-start(bf16[2,256,512]{1,2,0:T(8,128)(2,1)} %fusion.83), channel_id=1, source_target_pairs={{0,8},{8,16},{16,24},{24,32},{32,40},{40,48},{48,56},{56,64},{64,7... | collective-permute-start | bytes 1572872 | tf_op jit(solution)/shard_map/ppermute | solution.py:14
  163.0 5.8 %copy-start.5 = (bf16[256,4,128]{0,2,1:T(8,128)(2,1)S(1)}, bf16[256,4,128]{0,2,1:T(8,128)(2,1)}, u32[]{:S(2)}) copy-start(bf16[256,4,128]{0,2,1:T(8,128)(2,1)} %slice.216) | copy-start | bytes 786436
  169.6 15.5 %collective-permute-start.2 = (bf16[2,256,512]{1,2,0:T(8,128)(2,1)}, bf16[2,256,512]{1,2,0:T(8,128)(2,1)}, u32[]{:S(2)}, u32[]{:S(2)}) collective-permute-start(bf16[2,256,512]{1,2,0:T(8,128)(2,1)} %pad_maximum_fusion.6), channel_id=1, source_target_pairs={{8,0},{16,8},{24,16},{32,24},{40,32},{48,40},{56,48},{64,56},{72,6... | collective-permute-start | bytes 1572872 | tf_op jit(solution)/shard_map/ppermute | solution.py:14
  176.7 2.3 %copy-start.4 = (bf16[256,512]{1,0:T(8,128)(2,1)S(1)}, bf16[256,512]{1,0:T(8,128)(2,1)}, u32[]{:S(2)}) copy-start(bf16[256,512]{1,0:T(8,128)(2,1)} %copy.155) | copy-start | bytes 786436
  176.7 3.2 %copy-start.1 = (f32[256,4,128]{0,2,1:T(8,128)S(1)}, f32[256,4,128]{0,2,1:T(8,128)}, u32[]{:S(2)}) copy-start(f32[256,4,128]{0,2,1:T(8,128)} %get-tuple-element.187) | copy-start | bytes 1572868
  176.7 3.2 %copy-start.2 = (f32[256,4,128]{0,2,1:T(8,128)S(1)}, f32[256,4,128]{0,2,1:T(8,128)}, u32[]{:S(2)}) copy-start(f32[256,4,128]{0,2,1:T(8,128)} %get-tuple-element.189) | copy-start | bytes 1572868
  179.9 6.4 %copy-start = (f32[256,4,128]{0,2,1:T(8,128)S(1)}, f32[256,4,128]{0,2,1:T(8,128)}, u32[]{:S(2)}) copy-start(f32[256,4,128]{0,2,1:T(8,128)} %slice.190) | copy-start | bytes 1572868
  179.9 6.4 %slice-start = ((f32[512,4,128]{0,2,1:T(8,128)}), f32[256,4,128]{0,2,1:T(8,128)S(1)}, s32[]{:S(2)}) async-start(f32[512,4,128]{0,2,1:T(8,128)} %convolution_bitcast_fusion.3), calls=%async_computation.4 | async-start | bytes 1048576 | tf_op jit(solution)/shard_map/slice | solution.py:144
Sparse Core Ops, SparseCore 0:
  10.6 81.5 all-gather.1
  99.0 40.1 reduce-scatter.1
where the time goes:
time: 196 us; the launch traced here: 195 us
  waiting for transfers between devices  75.3 us (38%)
  matrix products  42.1 us (21%)
  local copies, waits for them, and re-layouts  32.6 us (17%)
  starting transfers between devices  21.4 us (11%)
  between operations  14.5 us (7%)
  other arithmetic  9.56 us (5%)
    all_gather x1, waiting for transfers between devices, local(): lax.all_gather(w_query, 'seq', axis=0, tiled=True)  69.5 us
    ppermute x4, starting transfers between devices, shifted(): return lax.ppermute(block, axis, route)  13.3 us
    dot_general x2, matrix products, one_step(): jnp.einsum('hqk,qhd->khd', grad_scores, query_heads, preferred_element_ty...  9.7 us
    dot_general x2, matrix products, one_step(): jnp.einsum('hqk,khd->qhd', grad_scores, key_heads, preferred_element_type...  8.45 us
    all_to_all x1, starting transfers between devices, local(): lax.all_to_all(buffer, 'seq', split_axis=1, concat_axis=1, tiled=True)  8.02 us
    dot_general x1, matrix products, local(): lax.dot_general(cross_dq, lax.all_gather(w_query, 'seq', axis=0, tiled=Tr...  6.66 us
    ppermute x4, waiting for transfers between devices, shifted(): return lax.ppermute(block, axis, route)  5.07 us
    dot_general x2, matrix products, one_step(): jnp.einsum('qhd,khd->hqk', dout_heads, value_heads, preferred_element_typ...  4.6 us
  transfers between devices with their start and end apart: 7, of which 2 were waited for; matrix products, arithmetic and copies ran while one was open for 43% of the time, Pallas kernels for 0%

commit v1 on v0

--- a/solution.py
+++ b/solution.py
@@ -3,6 +3,7 @@
 import jax.numpy as jnp
 from jax import lax
 from jax.sharding import PartitionSpec as P
+from jax.lax import all_to_all, axis_size
 
 HD = 128
 WIN = 256
@@ -105,6 +106,14 @@
     patch_owner,
     w_query,
 ):
+
+    def heads_derive(mat, mesh_name):
+        base_arr = all_to_all(
+            jnp.stack([mat for _ in range(axis_size(mesh_name))], axis=0), mesh_name, 0, 0
+        )
+        opened = jnp.concatenate(base_arr, 0)
+        return opened
+
     window = WIN
     row_count = win_query.shape[0]
     block_rows = row_count // 2
@@ -204,7 +213,7 @@
     patch_grads = arrived.reshape(2, seq_count * slot_cap, width)
     partial_sums = lax.dot_general(
         cross_dq,
-        lax.all_gather(w_query, "seq", axis=0, tiled=True),
+        heads_derive(w_query, "seq"),
         (((1,), (1,)), ((), ())),
         preferred_element_type=jnp.float32,
     )

time: 196 us -> 233 us (1.19)
  waiting for transfers between devices: 75.3 us -> 111 us
  starting transfers between devices: 21.4 us -> 28.5 us
  matrix products: 42.1 us -> 36.7 us
    all_to_all x0 -> x1, waiting for transfers between devices: none -> 90.7 us  [heads_derive(): all_to_all(jnp.stack([mat for _ in range(axis_size(mesh_name))], axis=0),...]
    all_gather x1 -> x0, waiting for transfers between devices: 69.5 us -> none  [local(): lax.all_gather(w_query, 'seq', axis=0, tiled=True)]
    ppermute x4, waiting for transfers between devices: 5.07 us -> 19.9 us  [shifted(): return lax.ppermute(block, axis, route)]
    all_to_all x0 -> x1, starting transfers between devices: none -> 10.4 us  [heads_derive(): all_to_all(jnp.stack([mat for _ in range(axis_size(mesh_name))], axis=0),...]
    another operation x0 -> x1, local copies, waits for them, and re-layouts: none -> 3.3 us  [heads_derive(): jnp.stack([mat for _ in range(axis_size(mesh_name))], axis=0)]
    ppermute x4, starting transfers between devices: 13.3 us -> 10.7 us  [shifted(): return lax.ppermute(block, axis, route)]
    unnamed x40 -> x42, local copies, waits for them, and re-layouts: 4.56 us -> 5.19 us
  transfers between devices with their start and end apart: 7 -> 7, of which waited for: 2 -> 3; matrix products, arithmetic and copies ran while one was open for 43% -> 29% of each run, Pallas kernels for 0% -> 0%
where the time goes in v1:
time: 233 us; the launch traced here: 232 us
  waiting for transfers between devices  111 us (48%)
  matrix products  36.7 us (16%)
  local copies, waits for them, and re-layouts  31.9 us (14%)
  starting transfers between devices  28.5 us (12%)
  between operations  14.5 us (6%)
  other arithmetic  9.57 us (4%)
    all_to_all x1, waiting for transfers between devices, heads_derive(): all_to_all(jnp.stack([mat for _ in range(axis_size(mesh_name))], axis=0),...  90.7 us
    ppermute x4, waiting for transfers between devices, shifted(): return lax.ppermute(block, axis, route)  19.9 us
    ppermute x4, starting transfers between devices, shifted(): return lax.ppermute(block, axis, route)  10.7 us
    all_to_all x1, starting transfers between devices, heads_derive(): all_to_all(jnp.stack([mat for _ in range(axis_size(mesh_name))], axis=0),...  10.4 us
    dot_general x2, matrix products, one_step(): jnp.einsum('hqk,qhd->khd', grad_scores, query_heads, preferred_element_ty...  9.63 us
    dot_general x2, matrix products, one_step(): jnp.einsum('hqk,khd->qhd', grad_scores, key_heads, preferred_element_type...  8.4 us
    all_to_all x1, starting transfers between devices, local(): lax.all_to_all(buffer, 'seq', split_axis=1, concat_axis=1, tiled=True)  7.41 us
    dot_general x1, matrix products, local(): lax.dot_general(cross_dq, heads_derive(w_query, 'seq'), (((1,), (1,)), ((...  6.5 us
  transfers between devices with their start and end apart: 7, of which 3 were waited for; matrix products, arithmetic and copies ran while one was open for 29% of the time, Pallas kernels for 0%

profile of v1, /device:TPU:102, one launch (start us, length us, event | category | flops | bytes accessed | tf_op | source)
XLA Modules:
  0.0 231.8 jit_solution(6609567802311444625)
XLA Ops:
  7.2 3.3 %stack.44 = bf16[32,128,512]{2,1,0:T(8,128)(2,1)} broadcast(bf16[128,512]{1,0:T(8,128)(2,1)} %param.37), dimensions={1,2} | broadcast | bytes 4325376 | tf_op jit(solution)/shard_map/stack | solution.py:112
  10.5 10.4 %all-to-all-start.1 = ((bf16[32,128,512]{2,1,0:T(8,128)(2,1)}), bf16[32,128,512]{2,1,0:T(8,128)(2,1)}, u32[]{:S(2)}, u32[]{:S(2)}) async-start(bf16[32,128,512]{2,1,0:T(8,128)(2,1)} %stack.44), calls=%async_computation.1 | async-start | bytes 8388608 | tf_op jit(solution)/shard_map/all_to_all | solution.py:111
  24.0 90.7 %all-to-all-done.1 = bf16[32,128,512]{2,1,0:T(8,128)(2,1)} async-done(((bf16[32,128,512]{2,1,0:T(8,128)(2,1)}), bf16[32,128,512]{2,1,0:T(8,128)(2,1)}, u32[]{:S(2)}, u32[]{:S(2)}) %all-to-all-start.1) | async-done | bytes 4194336 | tf_op jit(solution)/shard_map/all_to_all | solution.py:111
  114.7 6.5 %convolution_convert_fusion = bf16[512,4096]{1,0:T(8,128)(2,1)} fusion(bf16[4096,512]{1,0:T(8,128)(2,1)} %bitcast.48, bf16[64,8,4,128]{3,2,1,0:T(4,128)(2,1)S(1)} %bitcast.233), kind=kOutput, calls=%fused_computation.3 | convolution fusion | flops 2149580800 | bytes 8912896 | tf_op jit(solution)/shard_map/dot_general | solution.py:214
  122.9 0.9 copy.168
  123.8 7.4 %all-to-all-start = ((bf16[2,32,8,512]{3,2,0,1:T(8,128)(2,1)}), bf16[2,32,8,512]{3,2,0,1:T(8,128)(2,1)S(1)}, u32[]{:S(2)}, u32[]{:S(2)}) async-start(bf16[2,32,8,512]{3,2,0,1:T(8,128)(2,1)} %copy.168), calls=%async_computation | async-start | bytes 1048576 | tf_op jit(solution)/shard_map/all_to_all | solution.py:212
  131.6 0.8 pad_maximum_fusion.3
  132.5 2.8 %collective-permute-start.1 = (bf16[2,256,512]{1,2,0:T(8,128)(2,1)}, bf16[2,256,512]{1,2,0:T(8,128)(2,1)S(1)}, u32[]{:S(2)}, u32[]{:S(2)}) collective-permute-start(bf16[2,256,512]{1,2,0:T(8,128)(2,1)} %pad_maximum_fusion.3), channel_id=1, source_target_pairs={{8,0},{16,8},{24,16},{32,24},{40,32},{48,40},{56,48},{64,56},{72,6... | collective-permute-start | bytes 1572872 | tf_op jit(solution)/shard_map/ppermute | solution.py:15
  135.2 1.1 fusion.169
  136.3 1.1 fusion.170
  137.4 0.9 copy.188
  138.2 0.8 copy.192
  139.2 0.8 copy.133
  140.1 0.9 copy.145
  141.1 0.8 copy.149
  141.9 0.8 copy.137
  143.9 12.9 %collective-permute-done.1 = bf16[2,256,512]{1,2,0:T(8,128)(2,1)S(1)} collective-permute-done((bf16[2,256,512]{1,2,0:T(8,128)(2,1)}, bf16[2,256,512]{1,2,0:T(8,128)(2,1)S(1)}, u32[]{:S(2)}, u32[]{:S(2)}) %collective-permute-start.1) | collective-permute-done | bytes 524320 | tf_op jit(solution)/shard_map/ppermute | solution.py:15
  156.8 0.9 pad_maximum_fusion.1
  157.7 0.8 copy.144
  158.5 0.8 copy.148
  159.4 2.1 collective-permute-start
  161.5 1.6 fusion.6
  163.6 1.8 fusion.98
  165.4 1.7 convolution_bitcast_fusion
  167.1 3.8 %convolution_convert_fusion.3 = bf16[4,256,128]{1,2,0:T(8,128)(2,1)S(1)} fusion(f32[4,512,256]{2,1,0:T(8,128)} %fusion.98, f32[4,512,256]{2,1,0:T(8,128)S(1)} %get-tuple-element.206, f32[4,256]{1,0:T(4,128)S(1)} %log_add_fusion.1, pred[256,512]{0,1:T(8,128)(4,1)S(1)} %copy-done.3, bf16[256,4,128]{2,0,1:T(8,128)(2,1)} %copy.145, bf16[256,4,128]{2,0,1:T(8,128)(2,1)} %copy.144), kind=kOutput, calls=%fused_computation.45 | convolution fusion | flops 141166080 | bytes 5115904 | tf_op jit(solution)/shard_map/while/body/eval_jaxpr/hqk,khd->qhd/dot_general | solution.py:61
  170.9 0.9 copy.155
  171.7 2.1 fusion.166
  173.8 4.9 %convolution_bitcast_fusion.1 = f32[512,4,128]{0,2,1:T(8,128)} fusion(bf16[256,4,128]{0,2,1:T(8,128)(2,1)} %bitcast.237, f32[4,512,256]{2,1,0:T(8,128)} %fusion.98, f32[4,512,256]{2,1,0:T(8,128)S(1)} %get-tuple-element.206, f32[4,256]{1,0:T(4,128)S(1)} %log_add_fusion.1, pred[256,512]{0,1:T(8,128)(4,1)} %fusion.104), kind=kOutput, calls=%fused_computation.33 | convolution fusion | flops 139986432 | bytes 5640192 | tf_op jit(solution)/shard_map/while/body/eval_jaxpr/hqk,qhd->khd/dot_general | solution.py:64
  178.7 2.1 fusion.167
  180.8 0.9 fusion.83
  181.7 1.9 collective-permute-start.3
  184.4 1.8 fusion.168
  186.2 0.9 copy.132
  187.1 1.6 fusion.15
  190.6 0.8 slice.190
  191.4 1.8 copy.136
  193.2 2.8 %fusion.94 = f32[4,512,256]{2,1,0:T(8,128)} fusion(bf16[256,4,128]{0,2,1:T(8,128)(2,1)S(1)} %bitcast.223, bf16[256,4,128]{2,0,1:T(8,128)(2,1)} %copy.137, bf16[256,4,128]{2,0,1:T(8,128)(2,1)} %copy.136), kind=kOutput, calls=%fused_computation.107 | convolution fusion | flops 135266304 | bytes 2883584 | tf_op jit(solution)/shard_map/while/body/eval_jaxpr/qhd,khd->hqk/dot_general | solution.py:55
  196.0 4.7 %convolution_bitcast_fusion.3 = f32[512,4,128]{0,2,1:T(8,128)} fusion(bf16[256,4,128]{0,2,1:T(8,128)(2,1)} %bitcast.235, f32[4,512,256]{2,1,0:T(8,128)} %fusion.94, f32[4,512,256]{2,1,0:T(8,128)S(1)} %get-tuple-element.208, f32[4,256]{1,0:T(4,128)S(1)} %log_add_fusion.2, pred[256,512]{0,1:T(8,128)(4,1)S(1)} %broadcast_and_fusion), kind=kOutput, calls=%fused_computation.35 | convolution fusion | flops 139986432 | bytes 5640192 | tf_op jit(solution)/shard_map/while/body/eval_jaxpr/hqk,qhd->khd/dot_general | solution.py:64
  200.8 1.1 slice.217
  201.8 0.8 pad_maximum_fusion.6
  202.7 3.9 %collective-permute-start.2 = (bf16[2,256,512]{1,2,0:T(8,128)(2,1)}, bf16[2,256,512]{1,2,0:T(8,128)(2,1)}, u32[]{:S(2)}, u32[]{:S(2)}) collective-permute-start(bf16[2,256,512]{1,2,0:T(8,128)(2,1)} %pad_maximum_fusion.6), channel_id=1, source_target_pairs={{8,0},{16,8},{24,16},{32,24},{40,32},{48,40},{56,48},{64,56},{72,6... | collective-permute-start | bytes 1572872 | tf_op jit(solution)/shard_map/ppermute | solution.py:15
  206.6 4.6 %convolution_convert_fusion.4 = bf16[4,128,256]{2,1,0:T(8,128)(2,1)} fusion(f32[4,512,256]{2,1,0:T(8,128)} %fusion.94, f32[4,512,256]{2,1,0:T(8,128)S(1)} %get-tuple-element.208, f32[4,256]{1,0:T(4,128)S(1)} %log_add_fusion.2, pred[256,512]{0,1:T(8,128)(4,1)S(1)} %broadcast_and_fusion, bf16[256,4,128]{2,0,1:T(8,128)(2,1)} %copy.133, ...), kind=kOutput, calls=%fused_computation.46 | convolution fusion | flops 141166080 | bytes 5115904 | tf_op jit(solution)/shard_map/while/body/eval_jaxpr/hqk,khd->qhd/dot_general | solution.py:61
  211.2 1.2 copy.154
  212.4 1.1 convert_element_type.74
  214.6 7.0 %collective-permute-done.2 = bf16[2,256,512]{1,2,0:T(8,128)(2,1)} collective-permute-done((bf16[2,256,512]{1,2,0:T(8,128)(2,1)}, bf16[2,256,512]{1,2,0:T(8,128)(2,1)}, u32[]{:S(2)}, u32[]{:S(2)}) %collective-permute-start.2) | collective-permute-done | bytes 524320 | tf_op jit(solution)/shard_map/ppermute | solution.py:15
  221.6 1.1 select_add_fusion
  223.0 1.0 copy.172
  224.0 1.0 copy.173
  (87 shorter events, 11.0 us)
Async XLA Ops:
  10.5 10.5 %copy-start.14 = (s32[2,64]{1,0:T(2,128)S(1)}, s32[2,64]{1,0:T(2,128)}, u32[]{:S(2)}) copy-start(s32[2,64]{1,0:T(2,128)} %param.35) | copy-start | bytes 1540
  10.5 10.7 %copy-start.12 = (bf16[128,512]{1,0:T(8,128)(2,1)S(1)}, bf16[128,512]{1,0:T(8,128)(2,1)}, u32[]{:S(2)}) copy-start(bf16[128,512]{1,0:T(8,128)(2,1)} %param.33) | copy-start | bytes 393220
  10.5 10.8 %copy-start.13 = (bf16[128,512]{1,0:T(8,128)(2,1)S(1)}, bf16[128,512]{1,0:T(8,128)(2,1)}, u32[]{:S(2)}) copy-start(bf16[128,512]{1,0:T(8,128)(2,1)} %param.34) | copy-start | bytes 393220
  10.5 10.8 %copy-start.8 = (bf16[512,512]{1,0:T(8,128)(2,1)S(1)}, bf16[512,512]{1,0:T(8,128)(2,1)}, u32[]{:S(2)}) copy-start(bf16[512,512]{1,0:T(8,128)(2,1)} %param.31) | copy-start | bytes 1572868
  10.5 11.0 %copy-start.9 = (bf16[512,512]{1,0:T(8,128)(2,1)S(1)}, bf16[512,512]{1,0:T(8,128)(2,1)}, u32[]{:S(2)}) copy-start(bf16[512,512]{1,0:T(8,128)(2,1)} %param.32) | copy-start | bytes 1572868
  10.5 104.2 %all-to-all-start.1 = ((bf16[32,128,512]{2,1,0:T(8,128)(2,1)}), bf16[32,128,512]{2,1,0:T(8,128)(2,1)}, u32[]{:S(2)}, u32[]{:S(2)}) async-start(bf16[32,128,512]{2,1,0:T(8,128)(2,1)} %stack.44), calls=%async_computation.1 | async-start | bytes 8388608 | tf_op jit(solution)/shard_map/all_to_all | solution.py:111
  20.9 204.1 %reduce-scatter.2.cloned.1.call-start = ((), (), s32[]{:S(2)}) async-start(), calls=%async_computation.3 | async-start | bytes 4718592 | tf_op jit(solution)/shard_map/reduce_scatter | solution.py:220
  121.2 0.7 copy-start.15
  121.8 9.4 %copy-start.10 = (bf16[512,512]{1,0:T(8,128)(2,1)S(1)}, bf16[512,512]{1,0:T(8,128)(2,1)}, u32[]{:S(2)}) copy-start(bf16[512,512]{1,0:T(8,128)(2,1)} %param.28) | copy-start | bytes 1572868
  122.6 8.8 %copy-start.11 = (bf16[512,512]{1,0:T(8,128)(2,1)S(1)}, bf16[512,512]{1,0:T(8,128)(2,1)}, u32[]{:S(2)}) copy-start(bf16[512,512]{1,0:T(8,128)(2,1)} %param.29) | copy-start | bytes 1572868
  123.8 59.8 %all-to-all-start = ((bf16[2,32,8,512]{3,2,0,1:T(8,128)(2,1)}), bf16[2,32,8,512]{3,2,0,1:T(8,128)(2,1)S(1)}, u32[]{:S(2)}, u32[]{:S(2)}) async-start(bf16[2,32,8,512]{3,2,0,1:T(8,128)(2,1)} %copy.168), calls=%async_computation | async-start | bytes 1048576 | tf_op jit(solution)/shard_map/all_to_all | solution.py:212
  132.5 24.3 %collective-permute-start.1 = (bf16[2,256,512]{1,2,0:T(8,128)(2,1)}, bf16[2,256,512]{1,2,0:T(8,128)(2,1)S(1)}, u32[]{:S(2)}, u32[]{:S(2)}) collective-permute-start(bf16[2,256,512]{1,2,0:T(8,128)(2,1)} %pad_maximum_fusion.3), channel_id=1, source_target_pairs={{8,0},{16,8},{24,16},{32,24},{40,32},{48,40},{56,48},{64,56},{72,6... | collective-permute-start | bytes 1572872 | tf_op jit(solution)/shard_map/ppermute | solution.py:15
  157.6 3.8 %copy-start.3 = (pred[256,512]{0,1:T(8,128)(4,1)S(1)}, pred[256,512]{0,1:T(8,128)(4,1)}, u32[]{:S(2)}) copy-start(pred[256,512]{0,1:T(8,128)(4,1)} %fusion.104) | copy-start | bytes 393220
  159.4 25.1 %collective-permute-start = (bf16[2,256,512]{1,2,0:T(8,128)(2,1)}, bf16[2,256,512]{1,2,0:T(8,128)(2,1)}, u32[]{:S(2)}, u32[]{:S(2)}) collective-permute-start(bf16[2,256,512]{1,2,0:T(8,128)(2,1)} %get-tuple-element.195), channel_id=1, source_target_pairs={{0,8},{8,16},{16,24},{24,32},{32,40},{40,48},{48,56},{56,64},{64,7... | collective-permute-start | bytes 1572872 | tf_op jit(solution)/shard_map/ppermute | solution.py:15
  161.5 2.1 copy-start.6
  161.5 2.1 copy-start.7
  181.7 30.8 %collective-permute-start.3 = (bf16[2,256,512]{1,2,0:T(8,128)(2,1)}, bf16[2,256,512]{1,2,0:T(8,128)(2,1)}, u32[]{:S(2)}, u32[]{:S(2)}) collective-permute-start(bf16[2,256,512]{1,2,0:T(8,128)(2,1)} %fusion.83), channel_id=1, source_target_pairs={{0,8},{8,16},{16,24},{24,32},{32,40},{40,48},{48,56},{56,64},{64,7... | collective-permute-start | bytes 1572872 | tf_op jit(solution)/shard_map/ppermute | solution.py:15
  196.0 5.8 %copy-start.5 = (bf16[256,4,128]{0,2,1:T(8,128)(2,1)S(1)}, bf16[256,4,128]{0,2,1:T(8,128)(2,1)}, u32[]{:S(2)}) copy-start(bf16[256,4,128]{0,2,1:T(8,128)(2,1)} %slice.216) | copy-start | bytes 786436
  202.7 18.9 %collective-permute-start.2 = (bf16[2,256,512]{1,2,0:T(8,128)(2,1)}, bf16[2,256,512]{1,2,0:T(8,128)(2,1)}, u32[]{:S(2)}, u32[]{:S(2)}) collective-permute-start(bf16[2,256,512]{1,2,0:T(8,128)(2,1)} %pad_maximum_fusion.6), channel_id=1, source_target_pairs={{8,0},{16,8},{24,16},{32,24},{40,32},{48,40},{56,48},{64,56},{72,6... | collective-permute-start | bytes 1572872 | tf_op jit(solution)/shard_map/ppermute | solution.py:15
  211.2 2.3 %copy-start.4 = (bf16[256,512]{1,0:T(8,128)(2,1)S(1)}, bf16[256,512]{1,0:T(8,128)(2,1)}, u32[]{:S(2)}) copy-start(bf16[256,512]{1,0:T(8,128)(2,1)} %copy.155) | copy-start | bytes 786436
  211.2 3.2 %copy-start.1 = (f32[256,4,128]{0,2,1:T(8,128)S(1)}, f32[256,4,128]{0,2,1:T(8,128)}, u32[]{:S(2)}) copy-start(f32[256,4,128]{0,2,1:T(8,128)} %get-tuple-element.187) | copy-start | bytes 1572868
  211.2 3.2 %copy-start.2 = (f32[256,4,128]{0,2,1:T(8,128)S(1)}, f32[256,4,128]{0,2,1:T(8,128)}, u32[]{:S(2)}) copy-start(f32[256,4,128]{0,2,1:T(8,128)} %get-tuple-element.189) | copy-start | bytes 1572868
  214.4 8.3 %copy-start = (f32[256,4,128]{0,2,1:T(8,128)S(1)}, f32[256,4,128]{0,2,1:T(8,128)}, u32[]{:S(2)}) copy-start(f32[256,4,128]{0,2,1:T(8,128)} %slice.190) | copy-start | bytes 1572868
  214.4 8.3 %slice-start = ((f32[512,4,128]{0,2,1:T(8,128)}), f32[256,4,128]{0,2,1:T(8,128)S(1)}, s32[]{:S(2)}) async-start(f32[512,4,128]{0,2,1:T(8,128)} %convolution_bitcast_fusion.3), calls=%async_computation.4 | async-start | bytes 1048576 | tf_op jit(solution)/shard_map/slice | solution.py:153
Sparse Core Ops, SparseCore 0:
  121.3 40.2 reduce-scatter.1
